TPU v7x, 128 devices: a whole 4x4x4 slice. The times are simulated.
128 devices in a mesh: seq: 32 (over y, x, z_lo), tp: 4 (over z_hi, core).
Axes of the slice: x: 4, y: 4, z: 4 (z_hi: 2, z_lo: 2; z = z_hi * 2 + z_lo), core: 2. Of those that a mesh axis runs over, the one named last changes fastest.
Arguments:
- hidden_in: bfloat16 [24576, 4096], P(('seq', 'tp')), may hold values from -26 to 26
- norm_gain: float32 [4096], replicated, may hold values from 0.1 to 1.9
- w_qkv: bfloat16 [3, 4096, 2048], P(None, None, 'tp'), may hold values from -1 to 1
- w_out: bfloat16 [2048, 4096], P('tp'), may hold values from -0.125 to 0.125
Outputs:
- datastore: bfloat16 [24576, 4096], P(('seq', 'tp'))
All inputs are finite; a program needn't handle non-finite values.
Results may differ from a plain program's by a relative error of at most 0.006.
Values may be sent and summed in bfloat16 or wider, within the bound.
A program may use at most 128 MiB of HBM per device.

v0:
```python
import jax
import jax.numpy as jnp
from jax import lax
from jax.sharding import PartitionSpec as P

HD = 64
SPAN = 512
epsilon = 1e-06


def extended(block, sides, width):
    for axis, dim in sides:
        count = lax.axis_size(axis)
        forward = [(i, i + 1) for i in range(count - 1)]
        backward = [(target, source) for source, target in forward]
        low = lax.ppermute(
            lax.slice_in_dim(block, block.shape[dim] - width, None, axis=dim), axis, forward
        )
        high = lax.ppermute(lax.slice_in_dim(block, 0, width, axis=dim), axis, backward)
        block = jnp.concatenate([low, block, high], axis=dim)
    return block


def rms_scale(rows_in, norm_gain):
    widened = rows_in.astype(jnp.float32)
    mean_square = jnp.mean(widened * widened, axis=1, keepdims=True)
    return (widened * lax.rsqrt(mean_square + epsilon) * norm_gain[None, :]).astype(jnp.bfloat16)


def attend(queries, keys_pad, values_pad, at_start, at_end):
    span_len = SPAN
    half_len = span_len // 2
    quarter = span_len // 4
    query_rows = queries.shape[0]
    block_count = query_rows // half_len
    head_count = queries.shape[1] // HD
    query_blocks = queries.reshape(block_count, half_len, head_count, HD)
    key_blocks = jnp.stack(
        [
            keys_pad[number * half_len : number * half_len + span_len]
            for number in range(block_count)
        ]
    )
    value_blocks = jnp.stack(
        [
            values_pad[number * half_len : number * half_len + span_len]
            for number in range(block_count)
        ]
    )
    key_blocks = key_blocks.reshape(block_count, span_len, head_count, HD)
    value_blocks = value_blocks.reshape(block_count, span_len, head_count, HD)
    scores = jnp.einsum(
        "bqhd,bkhd->bhqk", query_blocks, key_blocks, preferred_element_type=jnp.float32
    )
    key_place = (
        jnp.arange(block_count, dtype=jnp.int32)[:, None] * half_len
        + jnp.arange(span_len, dtype=jnp.int32)[None, :]
    )
    left_out = jnp.logical_and(at_start, key_place < quarter)
    right_out = jnp.logical_and(at_end, key_place >= query_rows + quarter)
    key_valid = jnp.logical_not(jnp.logical_or(left_out, right_out))
    scores = jnp.where(key_valid[:, None, None, :], scores, -1e30)
    row_max = jnp.max(scores, axis=-1, keepdims=True)
    powers = jnp.exp(scores - row_max)
    weights = (powers / jnp.sum(powers, axis=-1, keepdims=True)).astype(jnp.bfloat16)
    context = jnp.einsum(
        "bhqk,bkhd->bqhd", weights, value_blocks, preferred_element_type=jnp.float32
    )
    return context.astype(jnp.bfloat16).reshape(query_rows, head_count * HD)


def on_device(hidden_in, norm_gain, w_qkv, w_out):
    seq_count = lax.axis_size("seq")
    seq_index = lax.axis_index("seq")
    own_rows = hidden_in.shape[0]
    model_width = hidden_in.shape[1]
    inner_width = w_qkv.shape[2]
    quarter = SPAN // 4
    at_start = seq_index == 0
    at_end = seq_index == seq_count - 1
    normed = lax.all_gather(rms_scale(hidden_in, norm_gain), "tp", axis=0, tiled=True)
    queries = jnp.dot(normed, w_qkv[0], preferred_element_type=jnp.float32).astype(jnp.bfloat16)
    keys_own = jnp.dot(normed, w_qkv[1], preferred_element_type=jnp.float32).astype(jnp.bfloat16)
    values_own = jnp.dot(normed, w_qkv[2], preferred_element_type=jnp.float32).astype(jnp.bfloat16)
    joined = jnp.concatenate([keys_own, values_own], axis=1)
    padded = extended(joined, (("seq", 0),), quarter)
    keys_pad = padded[:, :inner_width]
    values_pad = padded[:, inner_width:]
    context = attend(queries, keys_pad, values_pad, at_start, at_end)
    own_sum = lax.psum_scatter(
        jnp.dot(context, w_out, preferred_element_type=jnp.float32).astype(jnp.bfloat16),
        "tp",
        scatter_dimension=0,
        tiled=True,
    ).astype(jnp.float32)
    new_state = (hidden_in.astype(jnp.float32) + own_sum).astype(jnp.bfloat16)
    stripe_len = own_rows // seq_count
    pieces = new_state.reshape(seq_count, stripe_len, model_width)
    received = lax.all_to_all(pieces, "seq", split_axis=0, concat_axis=0, tiled=True)
    return received.reshape(own_rows, model_width)


def solution(mesh):
    return jax.shard_map(
        on_device,
        mesh=mesh,
        in_specs=(P(("seq", "tp"), None), P(), P(None, None, "tp"), P("tp", None)),
        out_specs=P(("seq", "tp"), None),
        check_vma=False,
    )
```

profile of v0, /device:TPU:0, one launch (start us, length us, event | category | flops | bytes accessed | tf_op | source)
XLA Modules:
  0.0 249.0 jit_solution(113620848852326442)
XLA Ops:
  6.5 0.0 all-gather.2.cloned.1.call-start
  6.5 1.8 fusion.16
  8.3 3.0 %fusion.18 = bf16[192,4096]{1,0:T(8,128)(2,1)} fusion(bf16[192,4096]{1,0:T(8,128)(2,1)} %param.4, f32[4096]{0:T(1024)} %param.5, f32[192]{0:T(256)S(1)} %add_rsqrt_fusion), kind=kLoop, calls=%fused_computation.23 | loop fusion | flops 3145728 | bytes 3162880 | tf_op jit(solution)/shard_map/convert_element_type | solution.py:27
  11.4 0.0 all-gather.2.cloned.1.call-update
  11.4 0.0 reduce-scatter.2.cloned.1.call-start
  11.5 0.1 fusion.52
  11.6 53.0 %all-gather.2.cloned.1.call-done = bf16[768,4096]{1,0:T(8,128)(2,1)} async-done(((bf16[192,4096]{1,0:T(8,128)(2,1)}), bf16[768,4096]{1,0:T(8,128)(2,1)}) %all-gather.2.cloned.1.call-update) | async-done | bytes 6291472 | tf_op jit(solution)/shard_map/all_gather | solution.py:81
  64.6 7.6 %fusion.35 = bf16[768,512]{0,1:T(8,128)(2,1)S(1)} fusion(bf16[768,4096]{1,0:T(8,128)(2,1)} %all-gather.2.cloned.1.call-done, bf16[3,4096,512]{2,1,0:T(8,128)(2,1)} %param.6), kind=kOutput, calls=%fused_computation.38 | convolution fusion | flops 3221618688 | bytes 11272192 | tf_op jit(solution)/shard_map/dot_general | solution.py:84
  72.2 0.0 copy-done.4
  72.2 5.9 %fusion.32 = bf16[768,512]{0,1:T(8,128)(2,1)S(1)} fusion(bf16[768,4096]{1,0:T(8,128)(2,1)S(1)} %copy-done.4, bf16[3,4096,512]{2,1,0:T(8,128)(2,1)} %param.6), kind=kOutput, calls=%fused_computation.37 | convolution fusion | flops 3221618688 | bytes 11272192 | tf_op jit(solution)/shard_map/dot_general | solution.py:83
  78.1 0.8 pad_maximum_fusion.7
  79.0 2.6 %collective-permute-start = (bf16[128,1024]{0,1:T(8,128)(2,1)}, bf16[128,1024]{0,1:T(8,128)(2,1)S(1)}, u32[]{:S(2)}, u32[]{:S(2)}) collective-permute-start(bf16[128,1024]{0,1:T(8,128)(2,1)} %get-tuple-element.11), channel_id=1, source_target_pairs={{0,4},{4,8},{8,12},{12,16},{16,20},{20,24},{24,28},{28,32},{32,36}... | collective-permute-start | bytes 786440 | tf_op jit(solution)/shard_map/ppermute | solution.py:16
  81.5 1.3 collective-permute-start.1
  82.8 6.5 %fusion.38 = bf16[768,512]{1,0:T(8,128)(2,1)} fusion(bf16[768,4096]{1,0:T(8,128)(2,1)S(1)} %copy-done.4, bf16[3,4096,512]{2,1,0:T(8,128)(2,1)} %param.6), kind=kOutput, calls=%fused_computation.39 | convolution fusion | flops 3221618688 | bytes 11272192 | tf_op jit(solution)/shard_map/dot_general | solution.py:82
  89.3 2.4 reshape.69
  91.8 1.6 collective-permute-done
  93.4 0.0 collective-permute-done.1
  93.4 2.2 pad_maximum_fusion.5
  95.6 6.3 %fusion.25 = f32[3,8,256,512]{3,2,1,0:T(8,128)} fusion(bf16[1,512,8,64]{1,3,2,0:T(8,128)(2,1)S(1)} %bitcast.35, bf16[1,512,8,64]{1,3,2,0:T(8,128)(2,1)S(1)} %bitcast.36, bf16[1,512,8,64]{1,3,2,0:T(8,128)(2,1)S(1)} %bitcast.34, bf16[3,256,8,64]{3,2,1,0:T(8,128)(2,1)S(1)} %reshape.69), kind=kOutput, calls=%fused_computation.30 | convolution fusion | flops 404226048 | bytes 14942208 | tf_op jit(solution)/shard_map/bqhd,bkhd->bhqk/dot_general | solution.py:52
  101.9 15.4 %fusion.56 = (f32[3,8,256]{2,1,0:T(8,128)S(1)}, f32[3,8,256,512]{3,2,1,0:T(8,128)}) fusion(f32[3,8,256,512]{3,2,1,0:T(8,128)} %fusion.25, pred[3,512]{1,0:T(4,128)(4,1)S(1)} %fusion.52), kind=kOutput, calls=%fused_computation.62 | output fusion | flops 12583423 | bytes 25191936 | tf_op jit(solution)/shard_map/sub | solution.py:64
  117.3 0.0 copy-done.3
  117.3 0.0 copy-start.5
  117.3 6.0 %fusion.44 = bf16[3,256,8,64]{1,3,2,0:T(8,128)(2,1)S(1)} fusion(f32[3,8,256,512]{3,2,1,0:T(8,128)} %get-tuple-element.16, f32[3,8,256]{2,1,0:T(8,128)S(1)} %get-tuple-element.15, bf16[1,512,8,64]{1,3,2,0:T(8,128)(2,1)S(1)} %bitcast.39, bf16[1,512,8,64]{1,3,2,0:T(8,128)(2,1)S(1)} %bitcast.40, bf16[1,512,8,64]{1,3,2,0:T(8,128)(2,1)S(1)} %bitcast.38), kind=kOutput, calls=%fused_computation.41 | convolution fusion | flops 410910720 | bytes 14966784 | tf_op jit(solution)/shard_map/bhqk,bkhd->bqhd/dot_general | solution.py:66
  123.3 0.7 copy.8
  123.9 0.2 copy.11
  124.1 5.4 %convolution_convert_fusion = bf16[768,4096]{1,0:T(8,128)(2,1)} fusion(bf16[768,512]{0,1:T(8,128)(2,1)S(1)} %bitcast.37, bf16[512,4096]{1,0:T(8,128)(2,1)S(1)} %copy-done.5), kind=kOutput, calls=%fused_computation.5 | convolution fusion | flops 3224371200 | bytes 11272192 | tf_op jit(solution)/shard_map/dot_general | solution.py:91
  129.5 0.0 reduce-scatter.2.cloned.1.call-update
  129.5 67.5 %reduce-scatter.2.cloned.1.call-done = bf16[192,4096]{1,0:T(8,128)(2,1)} async-done(((bf16[768,4096]{1,0:T(8,128)(2,1)}), bf16[192,4096]{1,0:T(8,128)(2,1)}) %reduce-scatter.2.cloned.1.call-update) | async-done | bytes 1572880 | tf_op jit(solution)/shard_map/reduce_scatter | solution.py:90
  197.0 3.1 %fusion.19 = bf16[192,4096]{1,0:T(8,128)(2,1)} fusion(bf16[192,4096]{1,0:T(8,128)(2,1)S(1)} %copy-done, bf16[192,4096]{1,0:T(8,128)(2,1)} %reduce-scatter.2.cloned.1.call-done), kind=kLoop, calls=%fused_computation.24 | loop fusion | flops 3145728 | bytes 4718592 | tf_op jit(solution)/shard_map/convert_element_type | solution.py:96
  200.1 2.4 reshape.67
  202.5 36.0 %all_to_all.5 = bf16[32,6,4096]{2,1,0:T(8,128)(2,1)} all-to-all(bf16[32,6,4096]{2,1,0:T(8,128)(2,1)S(1)} %reshape.67), channel_id=1, replica_groups=mesh['seq'=32,'tp'=4] {'seq'}, dimensions={0} | all-to-all | bytes 3145728 | tf_op jit(solution)/shard_map/all_to_all | solution.py:99
  238.5 3.7 %reshape.68 = bf16[192,4096]{1,0:T(8,128)(2,1)} reshape(bf16[32,6,4096]{2,1,0:T(8,128)(2,1)} %all_to_all.5) | data formatting | bytes 3145728 | tf_op jit(solution)/shard_map/reshape | solution.py:100
  (11 shorter events, 0.0 us)
Async XLA Ops:
  6.5 58.1 %all-gather.2.cloned.1.call-start = ((), (), s32[]{:S(2)}) async-start(), calls=%async_computation.2 | async-start | bytes 7864320 | tf_op jit(solution)/shard_map/all_gather | solution.py:81
  11.4 185.6 %reduce-scatter.2.cloned.1.call-start = ((), (), s32[]{:S(2)}) async-start(), calls=%async_computation.3 | async-start | bytes 7864320 | tf_op jit(solution)/shard_map/reduce_scatter | solution.py:90
  64.6 7.6 %copy-start.4 = (bf16[768,4096]{1,0:T(8,128)(2,1)S(1)}, bf16[768,4096]{1,0:T(8,128)(2,1)}, u32[]{:S(2)}) copy-start(bf16[768,4096]{1,0:T(8,128)(2,1)} %all-gather.2.cloned.1.call-done) | copy-start | bytes 18874372
  79.0 14.5 %collective-permute-start = (bf16[128,1024]{0,1:T(8,128)(2,1)}, bf16[128,1024]{0,1:T(8,128)(2,1)S(1)}, u32[]{:S(2)}, u32[]{:S(2)}) collective-permute-start(bf16[128,1024]{0,1:T(8,128)(2,1)} %get-tuple-element.11), channel_id=1, source_target_pairs={{0,4},{4,8},{8,12},{12,16},{16,20},{20,24},{24,28},{28,32},{32,36}... | collective-permute-start | bytes 786440 | tf_op jit(solution)/shard_map/ppermute | solution.py:16
  81.5 11.9 %collective-permute-start.1 = (bf16[128,1024]{0,1:T(8,128)(2,1)}, bf16[128,1024]{0,1:T(8,128)(2,1)}, u32[]{:S(2)}, u32[]{:S(2)}) collective-permute-start(bf16[128,1024]{0,1:T(8,128)(2,1)} %get-tuple-element.12), channel_id=1, source_target_pairs={{4,0},{8,4},{12,8},{16,12},{20,16},{24,20},{28,24},{32,28},{36,32}... | collective-permute-start | bytes 786440 | tf_op jit(solution)/shard_map/ppermute | solution.py:19
  101.9 15.4 %copy-start.1 = (bf16[512,512]{0,1:T(8,128)(2,1)S(1)}, bf16[512,512]{0,1:T(8,128)(2,1)}, u32[]{:S(2)}) copy-start(bf16[512,512]{0,1:T(8,128)(2,1)} %get-tuple-element.5) | copy-start | bytes 1572868
  101.9 15.4 %copy-start.2 = (bf16[512,512]{0,1:T(8,128)(2,1)S(1)}, bf16[512,512]{0,1:T(8,128)(2,1)}, u32[]{:S(2)}) copy-start(bf16[512,512]{0,1:T(8,128)(2,1)} %get-tuple-element.10) | copy-start | bytes 1572868
  101.9 15.4 %copy-start.3 = (bf16[512,512]{0,1:T(8,128)(2,1)S(1)}, bf16[512,512]{0,1:T(8,128)(2,1)}, u32[]{:S(2)}) copy-start(bf16[512,512]{0,1:T(8,128)(2,1)} %get-tuple-element.14) | copy-start | bytes 1572868
  117.3 6.8 %copy-start.5 = (bf16[512,4096]{1,0:T(8,128)(2,1)S(1)}, bf16[512,4096]{1,0:T(8,128)(2,1)}, u32[]{:S(2)}) copy-start(bf16[512,4096]{1,0:T(8,128)(2,1)} %param.7) | copy-start | bytes 12582916
  129.5 67.5 %copy-start = (bf16[192,4096]{1,0:T(8,128)(2,1)S(1)}, bf16[192,4096]{1,0:T(8,128)(2,1)}, u32[]{:S(2)}) copy-start(bf16[192,4096]{1,0:T(8,128)(2,1)} %param.4) | copy-start | bytes 4718596
Sparse Core Ops, SparseCore 0:
  11.5 53.0 all-gather.1
  129.6 67.2 reduce-scatter.1
where the time goes:
time: 250 us; the launch traced here: 249 us
  waiting for transfers between devices  122 us (49%)
  matrix products  37.6 us (15%)
  blocking collectives  36 us (14%)
  other arithmetic  26.4 us (11%)
  between operations  13.5 us (5%)
  local copies, waits for them, and re-layouts  9.4 us (4%)
  starting transfers between devices  3.9 us (2%)
    reduce_scatter x1, waiting for transfers between devices, on_device(): lax.psum_scatter(jnp.dot(context, w_out, preferred_element_type=jnp.float...  67.5 us
    all_gather x1, waiting for transfers between devices, on_device(): lax.all_gather(rms_scale(hidden_in, norm_gain), 'tp', axis=0, tiled=True)  53 us
    all_to_all x1, blocking collectives, on_device(): lax.all_to_all(pieces, 'seq', split_axis=0, concat_axis=0, tiled=True)  36 us
    sub x1, other arithmetic, attend(): powers = jnp.exp(scores - row_max)  15.4 us
    dot_general x1, matrix products, on_device(): jnp.dot(normed, w_qkv[2], preferred_element_type=jnp.float32)  7.61 us
    dot_general x1, matrix products, on_device(): jnp.dot(normed, w_qkv[0], preferred_element_type=jnp.float32)  6.49 us
    dot_general x1, matrix products, attend(): jnp.einsum('bqhd,bkhd->bhqk', query_blocks, key_blocks, preferred_element...  6.26 us
    dot_general x1, matrix products, attend(): jnp.einsum('bhqk,bkhd->bqhd', weights, value_blocks, preferred_element_ty...  5.96 us
  transfers between devices with their start and end apart: 4, of which 3 were waited for; matrix products, arithmetic and copies ran while one was open for 4% of the time, Pallas kernels for 0%

commit v1 on v0

--- a/solution.py
+++ b/solution.py
@@ -78,7 +78,12 @@
     quarter = SPAN // 4
     at_start = seq_index == 0
     at_end = seq_index == seq_count - 1
-    normed = lax.all_gather(rms_scale(hidden_in, norm_gain), "tp", axis=0, tiled=True)
+    normed = jnp.concatenate(
+        lax.all_to_all(
+            jnp.stack([rms_scale(hidden_in, norm_gain)] * lax.axis_size("tp")), "tp", 0, 0
+        ),
+        axis=0,
+    )
     queries = jnp.dot(normed, w_qkv[0], preferred_element_type=jnp.float32).astype(jnp.bfloat16)
     keys_own = jnp.dot(normed, w_qkv[1], preferred_element_type=jnp.float32).astype(jnp.bfloat16)
     values_own = jnp.dot(normed, w_qkv[2], preferred_element_type=jnp.float32).astype(jnp.bfloat16)

time: 250 us -> 279 us (1.12)
  waiting for transfers between devices: 122 us -> 139 us
  starting transfers between devices: 3.9 us -> 10.4 us
  local copies, waits for them, and re-layouts: 9.4 us -> 12.8 us
  matrix products: 37.6 us -> 40.8 us
    all_to_all x0 -> x1, waiting for transfers between devices: none -> 72.2 us  [on_device(): lax.all_to_all(jnp.stack([rms_scale(hidden_in, norm_gain)] * lax.axis_siz...]
    all_gather x1 -> x0, waiting for transfers between devices: 53 us -> none  [on_device(): lax.all_gather(rms_scale(hidden_in, norm_gain), 'tp', axis=0, tiled=True)]
    all_to_all x0 -> x1, starting transfers between devices: none -> 5.26 us  [on_device(): lax.all_to_all(jnp.stack([rms_scale(hidden_in, norm_gain)] * lax.axis_siz...]
    another operation x0 -> x1, local copies, waits for them, and re-layouts: none -> 3.43 us  [on_device(): jnp.stack([rms_scale(hidden_in, norm_gain)] * lax.axis_size('tp'))]
  transfers between devices with their start and end apart: 4 -> 4, of which waited for: 3 -> 2; matrix products, arithmetic and copies ran while one was open for 4% -> 4% of each run, Pallas kernels for 0% -> 0%
where the time goes in v1:
time: 279 us; the launch traced here: 278 us
  waiting for transfers between devices  139 us (50%)
  matrix products  40.8 us (15%)
  blocking collectives  36 us (13%)
  other arithmetic  25.3 us (9%)
  between operations  13.5 us (5%)
  local copies, waits for them, and re-layouts  12.8 us (5%)
  starting transfers between devices  10.4 us (4%)
    all_to_all x1, waiting for transfers between devices, on_device(): lax.all_to_all(jnp.stack([rms_scale(hidden_in, norm_gain)] * lax.axis_siz...  72.2 us
    reduce_scatter x1, waiting for transfers between devices, on_device(): lax.psum_scatter(jnp.dot(context, w_out, preferred_element_type=jnp.float...  67.3 us
    all_to_all x1, blocking collectives, on_device(): lax.all_to_all(pieces, 'seq', split_axis=0, concat_axis=0, tiled=True)  36 us
    sub x1, other arithmetic, attend(): powers = jnp.exp(scores - row_max)  15.4 us
    dot_general x1, matrix products, on_device(): jnp.dot(normed, w_qkv[0], preferred_element_type=jnp.float32)  8.29 us
    dot_general x1, matrix products, on_device(): jnp.dot(normed, w_qkv[1], preferred_element_type=jnp.float32)  7.47 us
    dot_general x1, matrix products, on_device(): jnp.dot(normed, w_qkv[2], preferred_element_type=jnp.float32)  7.47 us
    dot_general x1, matrix products, attend(): jnp.einsum('bqhd,bkhd->bhqk', query_blocks, key_blocks, preferred_element...  6.25 us
  transfers between devices with their start and end apart: 4, of which 2 were waited for; matrix products, arithmetic and copies ran while one was open for 4% of the time, Pallas kernels for 0%

profile of v1, /device:TPU:0, one launch (start us, length us, event | category | flops | bytes accessed | tf_op | source)
XLA Modules:
  0.0 278.3 jit_solution(442021781067473934)
XLA Ops:
  6.5 1.8 fusion.16
  8.3 1.9 fusion.18
  10.2 3.4 %stack.31 = bf16[4,192,4096]{2,1,0:T(8,128)(2,1)} broadcast(bf16[192,4096]{1,0:T(8,128)(2,1)S(1)} %fusion.18), dimensions={1,2} | broadcast | bytes 7864320 | tf_op jit(solution)/shard_map/stack | solution.py:83
  13.7 5.3 %all-to-all-start = ((bf16[4,192,4096]{2,1,0:T(8,128)(2,1)}), bf16[4,192,4096]{2,1,0:T(8,128)(2,1)}, u32[]{:S(2)}, u32[]{:S(2)}) async-start(bf16[4,192,4096]{2,1,0:T(8,128)(2,1)} %stack.31), calls=%async_computation | async-start | bytes 12582912 | tf_op jit(solution)/shard_map/all_to_all | solution.py:82
  18.9 0.0 reduce-scatter.2.cloned.1.call-start
  19.0 0.1 fusion.52
  19.1 72.2 %all-to-all-done = bf16[4,192,4096]{2,1,0:T(8,128)(2,1)} async-done(((bf16[4,192,4096]{2,1,0:T(8,128)(2,1)}), bf16[4,192,4096]{2,1,0:T(8,128)(2,1)}, u32[]{:S(2)}, u32[]{:S(2)}) %all-to-all-start) | async-done | bytes 6291488 | tf_op jit(solution)/shard_map/all_to_all | solution.py:82
  91.3 7.5 %fusion.35 = bf16[768,512]{0,1:T(8,128)(2,1)S(1)} fusion(bf16[768,4096]{1,0:T(8,128)(2,1)} %bitcast, bf16[3,4096,512]{2,1,0:T(8,128)(2,1)} %param.6), kind=kOutput, calls=%fused_computation.38 | convolution fusion | flops 3221618688 | bytes 11272192 | tf_op jit(solution)/shard_map/dot_general | solution.py:89
  98.7 7.5 %fusion.32 = bf16[768,512]{0,1:T(8,128)(2,1)S(1)} fusion(bf16[768,4096]{1,0:T(8,128)(2,1)} %bitcast, bf16[3,4096,512]{2,1,0:T(8,128)(2,1)} %param.6), kind=kOutput, calls=%fused_computation.37 | convolution fusion | flops 3221618688 | bytes 11272192 | tf_op jit(solution)/shard_map/dot_general | solution.py:88
  106.2 0.8 pad_maximum_fusion.7
  107.1 3.8 %collective-permute-start = (bf16[128,1024]{0,1:T(8,128)(2,1)}, bf16[128,1024]{0,1:T(8,128)(2,1)S(1)}, u32[]{:S(2)}, u32[]{:S(2)}) collective-permute-start(bf16[128,1024]{0,1:T(8,128)(2,1)} %get-tuple-element.11), channel_id=1, source_target_pairs={{0,4},{4,8},{8,12},{12,16},{16,20},{20,24},{24,28},{28,32},{32,36}... | collective-permute-start | bytes 786440 | tf_op jit(solution)/shard_map/ppermute | solution.py:16
  110.8 1.3 collective-permute-start.1
  112.1 8.3 %fusion.38 = bf16[768,512]{1,0:T(8,128)(2,1)} fusion(bf16[768,4096]{1,0:T(8,128)(2,1)} %bitcast, bf16[3,4096,512]{2,1,0:T(8,128)(2,1)} %param.6), kind=kOutput, calls=%fused_computation.39 | convolution fusion | flops 3221618688 | bytes 11272192 | tf_op jit(solution)/shard_map/dot_general | solution.py:87
  120.4 2.4 reshape.75
  122.9 0.0 collective-permute-done
  122.9 0.0 collective-permute-done.1
  122.9 2.2 pad_maximum_fusion.5
  125.1 6.3 %fusion.25 = f32[3,8,256,512]{3,2,1,0:T(8,128)} fusion(bf16[1,512,8,64]{1,3,2,0:T(8,128)(2,1)S(1)} %bitcast.36, bf16[1,512,8,64]{1,3,2,0:T(8,128)(2,1)S(1)} %bitcast.37, bf16[1,512,8,64]{1,3,2,0:T(8,128)(2,1)S(1)} %bitcast.35, bf16[3,256,8,64]{3,2,1,0:T(8,128)(2,1)S(1)} %reshape.75), kind=kOutput, calls=%fused_computation.30 | convolution fusion | flops 404226048 | bytes 14942208 | tf_op jit(solution)/shard_map/bqhd,bkhd->bhqk/dot_general | solution.py:52
  131.4 15.4 %fusion.56 = (f32[3,8,256]{2,1,0:T(8,128)S(1)}, f32[3,8,256,512]{3,2,1,0:T(8,128)}) fusion(f32[3,8,256,512]{3,2,1,0:T(8,128)} %fusion.25, pred[3,512]{1,0:T(4,128)(4,1)S(1)} %fusion.52), kind=kOutput, calls=%fused_computation.62 | output fusion | flops 12583423 | bytes 25191936 | tf_op jit(solution)/shard_map/sub | solution.py:64
  146.8 0.0 copy-done.1
  146.8 0.0 copy-done.3
  146.8 0.0 copy-start.4
  146.8 6.0 %fusion.44 = bf16[3,256,8,64]{1,3,2,0:T(8,128)(2,1)S(1)} fusion(f32[3,8,256,512]{3,2,1,0:T(8,128)} %get-tuple-element.16, f32[3,8,256]{2,1,0:T(8,128)S(1)} %get-tuple-element.15, bf16[1,512,8,64]{1,3,2,0:T(8,128)(2,1)S(1)} %bitcast.40, bf16[1,512,8,64]{1,3,2,0:T(8,128)(2,1)S(1)} %bitcast.41, bf16[1,512,8,64]{1,3,2,0:T(8,128)(2,1)S(1)} %bitcast.39), kind=kOutput, calls=%fused_computation.41 | convolution fusion | flops 410910720 | bytes 14966784 | tf_op jit(solution)/shard_map/bhqk,bkhd->bqhd/dot_general | solution.py:66
  152.8 0.7 copy.8
  153.4 0.2 copy.11
  153.6 5.4 %convolution_convert_fusion = bf16[768,4096]{1,0:T(8,128)(2,1)} fusion(bf16[768,512]{0,1:T(8,128)(2,1)S(1)} %bitcast.38, bf16[512,4096]{1,0:T(8,128)(2,1)S(1)} %copy-done.4), kind=kOutput, calls=%fused_computation.5 | convolution fusion | flops 3224371200 | bytes 11272192 | tf_op jit(solution)/shard_map/dot_general | solution.py:96
  159.0 0.0 reduce-scatter.2.cloned.1.call-update
  159.0 67.3 %reduce-scatter.2.cloned.1.call-done = bf16[192,4096]{1,0:T(8,128)(2,1)} async-done(((bf16[768,4096]{1,0:T(8,128)(2,1)}), bf16[192,4096]{1,0:T(8,128)(2,1)}) %reduce-scatter.2.cloned.1.call-update) | async-done | bytes 1572880 | tf_op jit(solution)/shard_map/reduce_scatter | solution.py:95
  226.3 3.1 %fusion.19 = bf16[192,4096]{1,0:T(8,128)(2,1)} fusion(bf16[192,4096]{1,0:T(8,128)(2,1)S(1)} %copy-done, bf16[192,4096]{1,0:T(8,128)(2,1)} %reduce-scatter.2.cloned.1.call-done), kind=kLoop, calls=%fused_computation.24 | loop fusion | flops 3145728 | bytes 4718592 | tf_op jit(solution)/shard_map/convert_element_type | solution.py:101
  229.4 2.4 reshape.73
  231.8 36.0 %all_to_all.10 = bf16[32,6,4096]{2,1,0:T(8,128)(2,1)} all-to-all(bf16[32,6,4096]{2,1,0:T(8,128)(2,1)S(1)} %reshape.73), channel_id=1, replica_groups=mesh['seq'=32,'tp'=4] {'seq'}, dimensions={0} | all-to-all | bytes 3145728 | tf_op jit(solution)/shard_map/all_to_all | solution.py:104
  267.8 3.7 %reshape.74 = bf16[192,4096]{1,0:T(8,128)(2,1)} reshape(bf16[32,6,4096]{2,1,0:T(8,128)(2,1)} %all_to_all.10) | data formatting | bytes 3145728 | tf_op jit(solution)/shard_map/reshape | solution.py:105
  (9 shorter events, 0.0 us)
Async XLA Ops:
  13.7 77.6 %all-to-all-start = ((bf16[4,192,4096]{2,1,0:T(8,128)(2,1)}), bf16[4,192,4096]{2,1,0:T(8,128)(2,1)}, u32[]{:S(2)}, u32[]{:S(2)}) async-start(bf16[4,192,4096]{2,1,0:T(8,128)(2,1)} %stack.31), calls=%async_computation | async-start | bytes 12582912 | tf_op jit(solution)/shard_map/all_to_all | solution.py:82
  18.9 207.4 %reduce-scatter.2.cloned.1.call-start = ((), (), s32[]{:S(2)}) async-start(), calls=%async_computation.3 | async-start | bytes 7864320 | tf_op jit(solution)/shard_map/reduce_scatter | solution.py:95
  107.1 15.8 %collective-permute-start = (bf16[128,1024]{0,1:T(8,128)(2,1)}, bf16[128,1024]{0,1:T(8,128)(2,1)S(1)}, u32[]{:S(2)}, u32[]{:S(2)}) collective-permute-start(bf16[128,1024]{0,1:T(8,128)(2,1)} %get-tuple-element.11), channel_id=1, source_target_pairs={{0,4},{4,8},{8,12},{12,16},{16,20},{20,24},{24,28},{28,32},{32,36}... | collective-permute-start | bytes 786440 | tf_op jit(solution)/shard_map/ppermute | solution.py:16
  110.8 12.1 %collective-permute-start.1 = (bf16[128,1024]{0,1:T(8,128)(2,1)}, bf16[128,1024]{0,1:T(8,128)(2,1)}, u32[]{:S(2)}, u32[]{:S(2)}) collective-permute-start(bf16[128,1024]{0,1:T(8,128)(2,1)} %get-tuple-element.12), channel_id=1, source_target_pairs={{4,0},{8,4},{12,8},{16,12},{20,16},{24,20},{28,24},{32,28},{36,32}... | collective-permute-start | bytes 786440 | tf_op jit(solution)/shard_map/ppermute | solution.py:19
  131.4 15.4 %copy-start.1 = (bf16[512,512]{0,1:T(8,128)(2,1)S(1)}, bf16[512,512]{0,1:T(8,128)(2,1)}, u32[]{:S(2)}) copy-start(bf16[512,512]{0,1:T(8,128)(2,1)} %get-tuple-element.5) | copy-start | bytes 1572868
  131.4 15.4 %copy-start.2 = (bf16[512,512]{0,1:T(8,128)(2,1)S(1)}, bf16[512,512]{0,1:T(8,128)(2,1)}, u32[]{:S(2)}) copy-start(bf16[512,512]{0,1:T(8,128)(2,1)} %get-tuple-element.10) | copy-start | bytes 1572868
  131.4 15.4 %copy-start.3 = (bf16[512,512]{0,1:T(8,128)(2,1)S(1)}, bf16[512,512]{0,1:T(8,128)(2,1)}, u32[]{:S(2)}) copy-start(bf16[512,512]{0,1:T(8,128)(2,1)} %get-tuple-element.14) | copy-start | bytes 1572868
  146.8 6.8 %copy-start.4 = (bf16[512,4096]{1,0:T(8,128)(2,1)S(1)}, bf16[512,4096]{1,0:T(8,128)(2,1)}, u32[]{:S(2)}) copy-start(bf16[512,4096]{1,0:T(8,128)(2,1)} %param.7) | copy-start | bytes 12582916
  159.0 67.3 %copy-start = (bf16[192,4096]{1,0:T(8,128)(2,1)S(1)}, bf16[192,4096]{1,0:T(8,128)(2,1)}, u32[]{:S(2)}) copy-start(bf16[192,4096]{1,0:T(8,128)(2,1)} %param.4) | copy-start | bytes 4718596
Sparse Core Ops, SparseCore 0:
  159.1 67.1 reduce-scatter.1
